TPU v7x, 256 devices: a whole 4x4x8 slice. The times are simulated.
256 devices in a mesh: unit: 16 (over x, z_lo), day: 16 (over y, z_hi, core).
Axes of the slice: x: 4, y: 4, z: 8 (z_hi: 2, z_lo: 4; z = z_hi * 4 + z_lo), core: 2. Of those that a mesh axis runs over, the one named last changes fastest.
Arguments:
- outcomes: float32 [65536, 4096], P('unit', 'day'), may hold values from -6 to 6
- cohort: int32 [65536], P('unit'), may hold values from 0 to 8
- pre_end: int32 [8], replicated, may hold values from 1024 to 2047
- post_start: int32 [8], replicated, may hold values from 2048 to 3071
- unit_logit: float32 [8, 65536], P(None, 'unit'), may hold values from -4 to 4
- time_logit: float32 [8, 4096], P(None, 'day'), may hold values from -4 to 4
Outputs:
- unit_weights: float32 [8, 65536], P(None, 'unit')
- time_weights: float32 [8, 4096], P(None, 'day')
All inputs are finite; a program needn't handle non-finite values.
Results may differ from a plain program's by a relative error of at most 0.0003.
Values sent between devices are 32-bit elements; how exact they have to be, the bound alone decides.
A program may use at most 64 MiB of HBM per device.

v0:
```python
import jax
import jax.numpy as jnp
from jax import lax
from jax.sharding import PartitionSpec as P

highest = lax.Precision.HIGHEST
step_rate = 16.0


def weigh_rows(left, outcomes):
    return jnp.dot(left, outcomes, precision=highest, preferred_element_type=jnp.float32)


def weigh_days(left, outcomes):
    return lax.dot_general(
        left,
        outcomes,
        (((1,), (1,)), ((), ())),
        precision=highest,
        preferred_element_type=jnp.float32,
    )


def local(outcomes, cohort, pre_end, post_start, unit_logit, time_logit):
    groups = pre_end.shape[0]
    unit_rows, day_cols = outcomes.shape
    day_devices = lax.axis_size("day")
    all_count = day_devices * day_cols
    labels = jnp.arange(groups, dtype=jnp.int32)[:, None]
    treated = (cohort[None, :] == labels).astype(jnp.float32)
    control = (cohort[None, :] > labels).astype(jnp.float32)
    day_start = lax.axis_index("day") * day_cols
    day_index = day_start + jnp.arange(day_cols, dtype=jnp.int32)[None, :]
    before = (day_index < pre_end[:, None]).astype(jnp.float32)
    before_len = pre_end.astype(jnp.float32)
    after_len = (all_count - post_start).astype(jnp.float32)
    raised = jnp.exp(unit_logit) * control
    unit_norm, treat_count, ctrl_count = lax.psum(
        (jnp.sum(raised, axis=1), jnp.sum(treated, axis=1), jnp.sum(control, axis=1)), "unit"
    )
    weights = raised / unit_norm[:, None]
    fitted, treat_sum = lax.psum(
        (weigh_rows(weights, outcomes), weigh_rows(treated, outcomes)), "unit"
    )
    residual = (fitted - treat_sum / jnp.maximum(treat_count, 1.0)[:, None]) * before
    ctrl_root = jnp.sqrt(jnp.maximum(ctrl_count, 1.0))[:, None]
    relaid = lax.all_to_all(outcomes, "day", split_axis=0, concat_axis=1, tiled=True)
    slab_rows = unit_rows // day_devices
    full_resid, full_logit = (
        lax.all_gather(residual, "day", axis=1, tiled=True),
        lax.all_gather(time_logit, "day", axis=1, tiled=True),
    )
    all_days = jnp.arange(all_count, dtype=jnp.int32)[None, :]
    full_before = (all_days < pre_end[:, None]).astype(jnp.float32)
    full_after = (all_days >= post_start[:, None]).astype(jnp.float32)
    row_start = lax.axis_index("day") * slab_rows
    sub_control = lax.dynamic_slice_in_dim(control, row_start, slab_rows, 1)
    sub_weights = lax.dynamic_slice_in_dim(weights, row_start, slab_rows, 1)
    unit_grad = weigh_days(full_resid, relaid)
    updated = sub_weights * jnp.exp(-step_rate * unit_grad / jnp.sqrt(before_len)[:, None])
    unit_total = lax.psum(jnp.sum(updated, axis=1), ("unit", "day"))
    row_share = updated / unit_total[:, None] * ctrl_count[:, None]
    unit_weights = lax.all_gather(row_share, "day", axis=1, tiled=True)
    time_raised = jnp.exp(full_logit) * full_before
    time_lam = time_raised / jnp.sum(time_raised, axis=1)[:, None]
    time_fit = weigh_days(time_lam, relaid)
    post_sum = weigh_days(full_after, relaid)
    shortfall = (time_fit - post_sum / after_len[:, None]) * sub_control
    time_grad = lax.psum(weigh_rows(shortfall, relaid), ("unit", "day"))
    moved = time_lam * jnp.exp(-step_rate * time_grad / ctrl_root)
    full_weights = moved / jnp.sum(moved, axis=1)[:, None] * before_len[:, None]
    time_weights = lax.dynamic_slice_in_dim(full_weights, day_start, day_cols, 1)
    return (unit_weights, time_weights)


def solution(mesh):
    return jax.shard_map(
        local,
        mesh=mesh,
        in_specs=(P("unit", "day"), P("unit"), P(), P(), P(None, "unit"), P(None, "day")),
        out_specs=(P(None, "unit"), P(None, "day")),
        check_vma=False,
    )
```

profile of v0, /device:TPU:2, one launch (start us, length us, event | category | flops | bytes accessed | tf_op | source)
XLA Modules:
  0.0 549.0 jit_solution(5261238960471951254)
XLA Ops:
  7.2 0.0 copy-start.2
  7.2 0.0 copy-start.3
  7.2 0.0 copy-start.4
  7.2 11.4 %all-to-all-start = ((f32[16,256,256]{2,1,0:T(8,128)}), f32[16,256,256]{2,1,0:T(8,128)}, u32[]{:S(2)}, u32[]{:S(2)}) async-start(f32[16,256,256]{2,1,0:T(8,128)} %bitcast.16), calls=%async_computation | async-start | bytes 8388608 | tf_op jit(solution)/shard_map/all_to_all | solution.py:47
  18.6 0.0 all-reduce.3.cloned.1.call-start
  18.6 0.0 copy-done.2
  18.7 0.0 copy-done.3
  18.7 0.2 fusion.13
  18.9 123.0 %psum.49 = f32[8]{0:T(128)S(1)} all-reduce(f32[8]{0:T(128)S(1)} %get-tuple-element.4), channel_id=1, replica_groups=mesh['unit'=16,'day'=16] {'unit'}, use_global_device_ids=true, to_apply=%region_1.0 | all-reduce | flops 8 | bytes 64 | tf_op jit(solution)/shard_map/psum | solution.py:38
  141.9 0.0 copy-done.4
  141.9 0.0 copy-start.1
  141.9 0.0 copy-start.5
  141.9 0.0 copy-start.6
  141.9 3.8 fusion.5
  145.7 0.1 fusion.7
  145.8 0.0 copy-done.1
  145.9 1.7 fusion.19
  147.6 73.4 %all-reduce = (f32[8,256]{1,0:T(8,128)S(1)}, f32[8,256]{1,0:T(8,128)S(1)}, f32[8]{0:T(128)S(1)}, f32[8]{0:T(128)S(1)}) all-reduce(f32[8,256]{1,0:T(8,128)S(1)} %fusion.19, f32[8,256]{1,0:T(8,128)S(1)} %fusion.5, f32[8]{0:T(128)S(1)} %get-tuple-element.3, f32[8]{0:T(128)S(1)} %get-tuple-element.2), channel_id=1, replica_groups=mesh['unit'=16,'day'=16] {'unit'}, use_global_device_ids=true, to_apply=%region_2.0 | all-reduce | flops 4112 | bytes 32896 | tf_op jit(solution)/shard_map/psum | solution.py:42
  221.0 0.0 copy-done.5
  221.0 29.0 %all_gather.11 = f32[8,4096]{1,0:T(8,128)S(1)} all-gather(f32[8,256]{1,0:T(8,128)S(1)} %copy-done.5), channel_id=1, replica_groups=mesh['unit'=16,'day'=16] {'day'}, dimensions={1}, use_global_device_ids=true | all-gather | bytes 139264 | tf_op jit(solution)/shard_map/all_gather | solution.py:51
  250.0 0.1 subtract_select_fusion
  250.0 25.6 %all_gather.9 = f32[8,4096]{1,0:T(8,128)S(1)} all-gather(f32[8,256]{1,0:T(8,128)S(1)} %subtract_select_fusion), channel_id=1, replica_groups=mesh['unit'=16,'day'=16] {'day'}, dimensions={1}, use_global_device_ids=true | all-gather | bytes 139264 | tf_op jit(solution)/shard_map/all_gather | solution.py:50
  275.7 0.2 fusion.10
  275.9 0.0 copy-done.6
  276.0 0.0 all-to-all-done
  276.0 5.4 copy.8
  281.3 0.0 copy-start
  281.3 4.2 fusion.15
  285.5 0.0 copy-done
  285.5 1.5 fusion.1
  287.0 4.2 fusion.20
  291.2 0.0 all-reduce.3.cloned.1.call-update
  291.2 4.0 fusion.18
  295.3 79.1 %psum.53 = f32[8]{0:T(128)S(1)} all-reduce(f32[8]{0:T(128)S(1)} %get-tuple-element.11), channel_id=1, replica_groups=mesh['unit'=16,'day'=16] {'unit','day'}, use_global_device_ids=true, to_apply=%region_7.0 | all-reduce | flops 8 | bytes 64 | tf_op jit(solution)/shard_map/psum | solution.py:61
  374.3 0.1 divide_multiply_fusion
  374.4 30.3 %all_gather.10 = f32[8,4096]{1,0:T(8,128)S(1)} all-gather(f32[8,256]{1,0:T(8,128)S(1)} %divide_multiply_fusion), channel_id=1, replica_groups=mesh['unit'=16,'day'=16] {'day'}, dimensions={1}, use_global_device_ids=true | all-gather | bytes 139264 | tf_op jit(solution)/shard_map/all_gather | solution.py:63
  404.7 135.0 %all-reduce.3.cloned.1.call-done = f32[8,4096]{1,0:T(8,128)} async-done(((f32[8,4096]{1,0:T(8,128)}), f32[8,4096]{1,0:T(8,128)}) %all-reduce.3.cloned.1.call-update) | async-done | bytes 131088 | tf_op jit(solution)/shard_map/psum | solution.py:69
  539.7 1.1 fusion.17
  540.8 0.7 fusion.14
  541.5 0.7 copy.11
  (7 shorter events, 0.0 us)
Async XLA Ops:
  7.2 11.5 %copy-start.2 = (f32[8,4096]{1,0:T(8,128)S(1)}, f32[8,4096]{1,0:T(8,128)}, u32[]{:S(2)}) copy-start(f32[8,4096]{1,0:T(8,128)} %param.10) | copy-start | bytes 393220
  7.2 11.5 %copy-start.3 = (s32[4096]{0:T(1024)S(1)}, s32[4096]{0:T(1024)}, u32[]{:S(2)}) copy-start(s32[4096]{0:T(1024)} %param.7) | copy-start | bytes 49156
  7.2 134.7 %copy-start.4 = (s32[8]{0:T(128)S(1)}, s32[8]{0:T(128)}, u32[]{:S(2)}) copy-start(s32[8]{0:T(128)} %param.8) | copy-start | bytes 100
  7.2 268.8 %all-to-all-start = ((f32[16,256,256]{2,1,0:T(8,128)}), f32[16,256,256]{2,1,0:T(8,128)}, u32[]{:S(2)}, u32[]{:S(2)}) async-start(f32[16,256,256]{2,1,0:T(8,128)} %bitcast.16), calls=%async_computation | async-start | bytes 8388608 | tf_op jit(solution)/shard_map/all_to_all | solution.py:47
  18.6 521.1 %all-reduce.3.cloned.1.call-start = ((), (), s32[]{:S(2)}) async-start(), calls=%async_computation.1 | async-start | bytes 262144 | tf_op jit(solution)/shard_map/psum | solution.py:69
  141.9 3.9 copy-start.1
  141.9 79.1 %copy-start.5 = (f32[8,256]{1,0:T(8,128)S(1)}, f32[8,256]{1,0:T(8,128)}, u32[]{:S(2)}) copy-start(f32[8,256]{1,0:T(8,128)} %param.11) | copy-start | bytes 24580
  141.9 134.0 %copy-start.6 = (s32[8]{0:T(128)S(1)}, s32[8]{0:T(128)}, u32[]{:S(2)}) copy-start(s32[8]{0:T(128)} %param.9) | copy-start | bytes 100
  281.3 4.2 copy-start
Sparse Core Ops, SparseCore 0:
  291.3 248.2 all-reduce.2
where the time goes:
time: 549 us
  blocking collectives  360 us (66%)
  waiting for transfers between devices  135 us (25%)
  matrix products  19.4 us (4%)
  between operations  14.2 us (3%)
  starting transfers between devices  11.4 us (2%)
  local copies, waits for them, and re-layouts  6.05 us (1%)
    psum x1, waiting for transfers between devices, local(): time_grad = lax.psum(weigh_rows(shortfall, relaid), ('unit', 'day'))  135 us
    psum x1, blocking collectives, local(): lax.psum((jnp.sum(raised, axis=1), jnp.sum(treated, axis=1), jnp.sum(cont...  123 us
    psum x1, blocking collectives, local(): unit_total = lax.psum(jnp.sum(updated, axis=1), ('unit', 'day'))  79.1 us
    psum x1, blocking collectives, local(): lax.psum((weigh_rows(weights, outcomes), weigh_rows(treated, outcomes)),...  73.4 us
    all_gather x1, blocking collectives, local(): unit_weights = lax.all_gather(row_share, 'day', axis=1, tiled=True)  30.3 us
    all_gather x1, blocking collectives, local(): lax.all_gather(time_logit, 'day', axis=1, tiled=True)  29 us
    all_gather x1, blocking collectives, local(): lax.all_gather(residual, 'day', axis=1, tiled=True)  25.6 us
    all_to_all x1, starting transfers between devices, local(): lax.all_to_all(outcomes, 'day', split_axis=0, concat_axis=1, tiled=True)  11.4 us
  transfers between devices with their start and end apart: 2, of which 1 were waited for; matrix products, arithmetic and copies ran while one was open for 2% of the time, Pallas kernels for 0%

commit v1 on v0

--- a/solution.py
+++ b/solution.py
@@ -66,7 +66,9 @@
     time_fit = weigh_days(time_lam, relaid)
     post_sum = weigh_days(full_after, relaid)
     shortfall = (time_fit - post_sum / after_len[:, None]) * sub_control
-    time_grad = lax.psum(weigh_rows(shortfall, relaid), ("unit", "day"))
+    time_grad = weigh_rows(shortfall, relaid)
+    for tick in ("unit", "day"):
+        time_grad = lax.psum(time_grad, tick)
     moved = time_lam * jnp.exp(-step_rate * time_grad / ctrl_root)
     full_weights = moved / jnp.sum(moved, axis=1)[:, None] * before_len[:, None]
     time_weights = lax.dynamic_slice_in_dim(full_weights, day_start, day_cols, 1)

time: 549 us -> 644 us (1.17)
  waiting for transfers between devices: 135 us -> 227 us
    psum x1 -> x2, waiting for transfers between devices: 135 us -> 227 us  [local(): time_grad = lax.psum(time_grad, tick)]
  transfers between devices with their start and end apart: 2 -> 3, of which waited for: 1 -> 2; matrix products, arithmetic and copies ran while one was open for 2% -> 2% of each run, Pallas kernels for 0% -> 0%
where the time goes in v1:
time: 644 us; the launch traced here: 642 us
  blocking collectives  362 us (56%)
  waiting for transfers between devices  227 us (35%)
  matrix products  19.4 us (3%)
  between operations  14.2 us (2%)
  starting transfers between devices  11.7 us (2%)
    psum x2, waiting for transfers between devices, local(): time_grad = lax.psum(time_grad, tick)  227 us
    psum x1, blocking collectives, local(): lax.psum((jnp.sum(raised, axis=1), jnp.sum(treated, axis=1), jnp.sum(cont...  123 us
    psum x1, blocking collectives, local(): unit_total = lax.psum(jnp.sum(updated, axis=1), ('unit', 'day'))  79.4 us
    psum x1, blocking collectives, local(): lax.psum((weigh_rows(weights, outcomes), weigh_rows(treated, outcomes)),...  73.4 us
    all_gather x1, blocking collectives, local(): unit_weights = lax.all_gather(row_share, 'day', axis=1, tiled=True)  31.4 us
    all_gather x1, blocking collectives, local(): lax.all_gather(time_logit, 'day', axis=1, tiled=True)  29 us
    all_gather x1, blocking collectives, local(): lax.all_gather(residual, 'day', axis=1, tiled=True)  25.5 us
  transfers between devices with their start and end apart: 3, of which 2 were waited for; matrix products, arithmetic and copies ran while one was open for 2% of the time, Pallas kernels for 0%

profile of v1, /device:TPU:2, one launch (start us, length us, event | category | flops | bytes accessed | tf_op | source)
XLA Modules:
  0.0 642.2 jit_solution(14951598003741277257)
XLA Ops:
  7.2 0.0 copy-start.2
  7.2 0.0 copy-start.3
  7.2 0.0 copy-start.4
  7.2 11.4 %all-to-all-start = ((f32[16,256,256]{2,1,0:T(8,128)}), f32[16,256,256]{2,1,0:T(8,128)}, u32[]{:S(2)}, u32[]{:S(2)}) async-start(f32[16,256,256]{2,1,0:T(8,128)} %bitcast.16), calls=%async_computation | async-start | bytes 8388608 | tf_op jit(solution)/shard_map/all_to_all | solution.py:47
  18.6 0.0 all-reduce.4.cloned.1.call-start
  18.6 0.0 copy-done.2
  18.7 0.0 copy-done.3
  18.7 0.2 fusion.13
  18.9 123.0 %psum.56 = f32[8]{0:T(128)S(1)} all-reduce(f32[8]{0:T(128)S(1)} %get-tuple-element.4), channel_id=1, replica_groups=mesh['unit'=16,'day'=16] {'unit'}, use_global_device_ids=true, to_apply=%region_1.0 | all-reduce | flops 8 | bytes 64 | tf_op jit(solution)/shard_map/psum | solution.py:38
  141.9 0.0 copy-done.4
  141.9 0.0 copy-start.1
  141.9 0.0 copy-start.5
  141.9 0.0 copy-start.6
  141.9 3.8 fusion.5
  145.7 0.1 fusion.7
  145.8 0.0 copy-done.1
  145.9 1.7 fusion.19
  147.6 73.4 %all-reduce = (f32[8,256]{1,0:T(8,128)S(1)}, f32[8,256]{1,0:T(8,128)S(1)}, f32[8]{0:T(128)S(1)}, f32[8]{0:T(128)S(1)}) all-reduce(f32[8,256]{1,0:T(8,128)S(1)} %fusion.19, f32[8,256]{1,0:T(8,128)S(1)} %fusion.5, f32[8]{0:T(128)S(1)} %get-tuple-element.3, f32[8]{0:T(128)S(1)} %get-tuple-element.2), channel_id=1, replica_groups=mesh['unit'=16,'day'=16] {'unit'}, use_global_device_ids=true, to_apply=%region_2.0 | all-reduce | flops 4112 | bytes 32896 | tf_op jit(solution)/shard_map/psum | solution.py:42
  221.0 0.0 copy-done.5
  221.0 29.0 %all_gather.11 = f32[8,4096]{1,0:T(8,128)S(1)} all-gather(f32[8,256]{1,0:T(8,128)S(1)} %copy-done.5), channel_id=1, replica_groups=mesh['unit'=16,'day'=16] {'day'}, dimensions={1}, use_global_device_ids=true | all-gather | bytes 139264 | tf_op jit(solution)/shard_map/all_gather | solution.py:51
  250.0 0.1 subtract_select_fusion
  250.0 25.5 %all_gather.9 = f32[8,4096]{1,0:T(8,128)S(1)} all-gather(f32[8,256]{1,0:T(8,128)S(1)} %subtract_select_fusion), channel_id=1, replica_groups=mesh['unit'=16,'day'=16] {'day'}, dimensions={1}, use_global_device_ids=true | all-gather | bytes 139264 | tf_op jit(solution)/shard_map/all_gather | solution.py:50
  275.5 0.2 fusion.10
  275.7 0.0 copy-done.6
  275.8 0.0 all-to-all-done
  275.8 5.4 copy.8
  281.1 0.0 copy-start
  281.1 4.2 fusion.15
  285.3 0.0 copy-done
  285.3 1.5 fusion.1
  286.8 4.2 fusion.20
  291.0 0.0 all-reduce.4.cloned.1.call-update
  291.0 0.2 all-reduce.6.cloned.1.call-start
  291.3 4.0 fusion.18
  295.3 79.4 %psum.60 = f32[8]{0:T(128)S(1)} all-reduce(f32[8]{0:T(128)S(1)} %get-tuple-element.11), channel_id=1, replica_groups=mesh['unit'=16,'day'=16] {'unit','day'}, use_global_device_ids=true, to_apply=%region_7.0 | all-reduce | flops 8 | bytes 64 | tf_op jit(solution)/shard_map/psum | solution.py:61
  374.7 74.0 %all-reduce.4.cloned.1.call-done = f32[8,4096]{1,0:T(8,128)} async-done(((f32[8,4096]{1,0:T(8,128)}), f32[8,4096]{1,0:T(8,128)}) %all-reduce.4.cloned.1.call-update) | async-done | bytes 131088 | tf_op jit(solution)/shard_map/psum | solution.py:71
  448.8 0.0 all-reduce.6.cloned.1.call-update
  448.8 0.1 divide_multiply_fusion
  448.9 31.4 %all_gather.10 = f32[8,4096]{1,0:T(8,128)S(1)} all-gather(f32[8,256]{1,0:T(8,128)S(1)} %divide_multiply_fusion), channel_id=1, replica_groups=mesh['unit'=16,'day'=16] {'day'}, dimensions={1}, use_global_device_ids=true | all-gather | bytes 139264 | tf_op jit(solution)/shard_map/all_gather | solution.py:63
  480.2 152.7 %all-reduce.6.cloned.1.call-done = f32[8,4096]{1,0:T(8,128)} async-done(((f32[8,4096]{1,0:T(8,128)}), f32[8,4096]{1,0:T(8,128)}) %all-reduce.6.cloned.1.call-update) | async-done | bytes 131088 | tf_op jit(solution)/shard_map/psum | solution.py:71
  632.9 1.1 fusion.17
  634.0 0.7 fusion.14
  634.7 0.7 copy.12
  (7 shorter events, 0.0 us)
Async XLA Ops:
  7.2 11.5 %copy-start.2 = (f32[8,4096]{1,0:T(8,128)S(1)}, f32[8,4096]{1,0:T(8,128)}, u32[]{:S(2)}) copy-start(f32[8,4096]{1,0:T(8,128)} %param.10) | copy-start | bytes 393220
  7.2 11.5 %copy-start.3 = (s32[4096]{0:T(1024)S(1)}, s32[4096]{0:T(1024)}, u32[]{:S(2)}) copy-start(s32[4096]{0:T(1024)} %param.7) | copy-start | bytes 49156
  7.2 134.7 %copy-start.4 = (s32[8]{0:T(128)S(1)}, s32[8]{0:T(128)}, u32[]{:S(2)}) copy-start(s32[8]{0:T(128)} %param.8) | copy-start | bytes 100
  7.2 268.6 %all-to-all-start = ((f32[16,256,256]{2,1,0:T(8,128)}), f32[16,256,256]{2,1,0:T(8,128)}, u32[]{:S(2)}, u32[]{:S(2)}) async-start(f32[16,256,256]{2,1,0:T(8,128)} %bitcast.16), calls=%async_computation | async-start | bytes 8388608 | tf_op jit(solution)/shard_map/all_to_all | solution.py:47
  18.6 430.2 %all-reduce.4.cloned.1.call-start = ((), (), s32[]{:S(2)}) async-start(), calls=%async_computation.1 | async-start | bytes 262144 | tf_op jit(solution)/shard_map/psum | solution.py:71
  141.9 3.9 copy-start.1
  141.9 79.1 %copy-start.5 = (f32[8,256]{1,0:T(8,128)S(1)}, f32[8,256]{1,0:T(8,128)}, u32[]{:S(2)}) copy-start(f32[8,256]{1,0:T(8,128)} %param.11) | copy-start | bytes 24580
  141.9 133.8 %copy-start.6 = (s32[8]{0:T(128)S(1)}, s32[8]{0:T(128)}, u32[]{:S(2)}) copy-start(s32[8]{0:T(128)} %param.9) | copy-start | bytes 100
  281.1 4.2 copy-start
  291.0 341.9 %all-reduce.6.cloned.1.call-start = ((), (), s32[]{:S(2)}) async-start(), calls=%async_computation.2 | async-start | bytes 262144 | tf_op jit(solution)/shard_map/psum | solution.py:71
Sparse Core Ops, SparseCore 0:
  291.1 157.5 all-reduce.3
  451.4 181.4 all-reduce.5
